TPU v7x, 32 devices: a whole 2x2x4 slice. The times are simulated.
32 devices in a mesh: row: 4 (over z), col: 8 (over y, x, core).
Axes of the slice: x: 2, y: 2, z: 4, core: 2. Of those that a mesh axis runs over, the one named last changes fastest.
Arguments:
- src_points: bfloat16 [512, 32, 256], P('row'), may hold values from -6 to 6
- tgt_points: bfloat16 [64, 32, 256], P('col'), may hold values from -6 to 6
- log_src: float32 [512, 256], P('row'), may hold values from -4 to 4
- log_tgt: float32 [64, 256], P('col'), may hold values from -4 to 4
- tgt_potential: float32 [64, 256], P('col'), may hold values from -1 to 25
- pattern: int32 [512, 4], P('row'), may hold values from 0 to 63, as said below
Outputs:
- src_new: float32 [512, 256], P('row')
- tgt_new: float32 [64, 256], P('col')
Inputs may be any that keep to these rules, and one draw needn't show every extreme that they name: `pattern`: each row names 4 different target blocks. For every index of row and every index of col, at most 128 of the entries in that index's source blocks name a target block held by that index of col, and exactly 128 do for some index of col. Every target block is named by some entry.
All inputs are finite; a program needn't handle non-finite values.
Results may differ from a plain program's by a relative error of at most 0.0015.
Values may be sent and summed in bfloat16 or wider, within the bound.
No kernel may reach another device: no remote copies, remote signals or barrier semaphores. Data moves between devices by JAX's collectives and lax.ppermute only.
A program may use at most 64 MiB of HBM per device.

v0:
```python
import math
import jax
import jax.numpy as jnp
from jax import lax
from jax.sharding import PartitionSpec as P

DIM = 32
FANOUT = 4
PAIR_MEAN = 64
epsilon = 0.1
very_low = -1e30
entry_batch = 8


def joined(value, axis, join):
    pieces = jax.tree.map(lambda part: lax.all_gather(part, axis), value)
    head = jax.tree.map(lambda part: part[0], pieces)
    tail = jax.tree.map(lambda part: part[1:], pieces)
    subtotal, _ = lax.scan(lambda subtotal, share: (join(subtotal, share), None), head, tail)
    return subtotal


def merge_parts(left_part, right_part):
    top_score = jnp.maximum(left_part[0], right_part[0])
    exp_total = left_part[1] * jnp.exp(left_part[0] - top_score) + right_part[1] * jnp.exp(
        right_part[0] - top_score
    )
    return (top_score, exp_total)


def pick_rows(table, row_ids, precise):
    table_rows = table.shape[0]
    flat = table.reshape(table_rows, -1)
    selector = (row_ids[:, None] == jnp.arange(table_rows, dtype=jnp.int32)[None, :]).astype(
        flat.dtype
    )
    if precise:
        picked = jnp.dot(
            selector, flat, precision=lax.Precision.HIGHEST, preferred_element_type=jnp.float32
        )
    else:
        picked = jnp.dot(selector, flat, preferred_element_type=jnp.float32).astype(table.dtype)
    return picked.reshape((row_ids.shape[0],) + table.shape[1:])


def collect_rows(row_total_count, row_ids, part_top, part_total):
    group = math.gcd(row_total_count, 32)

    def group_top(first_row):
        group_ids = first_row + jnp.arange(group, dtype=jnp.int32)
        member = row_ids[None, :] == group_ids[:, None]
        return jnp.max(jnp.where(member[:, :, None], part_top[None, :, :], very_low), axis=1)

    starts = jnp.arange(0, row_total_count, group, dtype=jnp.int32)
    block_top = lax.map(group_top, starts).reshape(row_total_count, part_top.shape[1])
    picked_top = pick_rows(block_top, row_ids, True)
    member_all = (row_ids[None, :] == jnp.arange(row_total_count, dtype=jnp.int32)[:, None]).astype(
        jnp.float32
    )
    block_total = jnp.dot(
        member_all,
        part_total * jnp.exp(part_top - picked_top),
        precision=lax.Precision.HIGHEST,
        preferred_element_type=jnp.float32,
    )
    return (block_top, block_total)


def on_device(src_points, tgt_points, log_src, log_tgt, tgt_potential, pattern):
    cell_count = src_points.shape[2]
    col_index = lax.axis_index("col")
    flat_targets = pattern.reshape(-1)
    all_points = lax.all_gather(tgt_points, "col", axis=0, tiled=True)
    all_potential = lax.all_gather(tgt_potential, "col", axis=0, tiled=True)
    slot_count = PAIR_MEAN
    chosen = col_index * slot_count + jnp.arange(slot_count, dtype=jnp.int32)
    slot_src = chosen // FANOUT
    slot_tgt = lax.dynamic_slice_in_dim(flat_targets, col_index * slot_count, slot_count, 0)
    in_use = jnp.ones((slot_count,), jnp.bool_)
    turn_count = slot_count // entry_batch
    slot_src_points = pick_rows(src_points, slot_src, False)
    slot_tgt_points = pick_rows(all_points, slot_tgt, False)
    slot_potential = pick_rows(all_potential, slot_tgt, True)
    point_shape = (turn_count, entry_batch) + src_points.shape[1:]
    batches = (
        slot_src_points.reshape(point_shape),
        slot_tgt_points.reshape(point_shape),
        in_use.reshape(turn_count, entry_batch),
    )

    def distances(src_block, tgt_block):
        products = jnp.einsum(
            "gdi,gdj->gij", src_block, tgt_block, preferred_element_type=jnp.float32
        )
        src_square = jnp.sum(jnp.square(src_block.astype(jnp.float32)), axis=1)
        tgt_square = jnp.sum(jnp.square(tgt_block.astype(jnp.float32)), axis=1)
        return (src_square[:, :, None] + tgt_square[:, None, :] - 2.0 * products) / DIM

    def row_terms(costs, potential_rows, used):
        scores = (potential_rows[:, None, :] - costs) / epsilon
        top_score = jnp.max(scores, axis=2)
        exp_total = jnp.sum(jnp.exp(scores - top_score[:, :, None]), axis=2)
        top_score = jnp.where(used[:, None], top_score, very_low)
        exp_total = jnp.where(used[:, None], exp_total, 0.0)
        return (top_score, exp_total)

    row_batches = batches + (slot_potential.reshape(turn_count, entry_batch, cell_count),)

    def row_fresh(state_in, members):
        return (state_in, row_terms(distances(members[0], members[1]), members[3], members[2]))

    row_out = lax.scan(row_fresh, None, row_batches)[1]
    row_top = row_out[0].reshape(slot_count, cell_count)
    row_total = row_out[1].reshape(slot_count, cell_count)
    own_count = slot_count // FANOUT
    own_start = col_index * own_count
    own_top = jnp.max(row_top.reshape(own_count, FANOUT, cell_count), axis=1)
    own_total = jnp.sum(
        (row_total * jnp.exp(row_top - jnp.repeat(own_top, FANOUT, axis=0))).reshape(
            own_count, FANOUT, cell_count
        ),
        axis=1,
    )
    own_log = lax.dynamic_slice_in_dim(log_src, own_start, own_count, 0)
    own_new = epsilon * own_log - epsilon * (own_top + jnp.log(own_total))
    src_new = lax.all_gather(own_new, "col", axis=0, tiled=True)
    slot_src_new = pick_rows(src_new, slot_src, True).reshape(turn_count, entry_batch, cell_count)

    def column_terms(costs, src_rows, used):
        weights = (src_rows[:, :, None] - costs) / epsilon
        top_score = jnp.max(weights, axis=1)
        exp_total = jnp.sum(jnp.exp(weights - top_score[:, None, :]), axis=1)
        top_score = jnp.where(used[:, None], top_score, very_low)
        exp_total = jnp.where(used[:, None], exp_total, 0.0)
        return (top_score, exp_total)

    def column_fresh(state_in, members):
        return (state_in, column_terms(distances(members[0], members[1]), members[3], members[2]))

    column_out = lax.scan(column_fresh, None, batches + (slot_src_new,))[1]
    column_top = column_out[0].reshape(slot_count, cell_count)
    column_total = column_out[1].reshape(slot_count, cell_count)
    tgt_rows = all_points.shape[0]
    target_top, target_total = collect_rows(tgt_rows, slot_tgt, column_top, column_total)
    sent_top, sent_total = (
        lax.all_to_all(target_top[:, None, :], "col", split_axis=0, concat_axis=1, tiled=True),
        lax.all_to_all(target_total[:, None, :], "col", split_axis=0, concat_axis=1, tiled=True),
    )
    local_top = jnp.max(sent_top, axis=1)
    local_total = jnp.sum(sent_total * jnp.exp(sent_top - local_top[:, None, :]), axis=1)
    final_top, final_total = joined((local_top, local_total), "row", merge_parts)
    tgt_new = epsilon * log_tgt - epsilon * (final_top + jnp.log(final_total))
    return (src_new, tgt_new)


def solution(mesh):
    placed = (
        P("row", None, None),
        P("col", None, None),
        P("row", None),
        P("col", None),
        P("col", None),
        P("row", None),
    )
    return jax.shard_map(
        on_device,
        mesh=mesh,
        in_specs=placed,
        out_specs=(P("row", None), P("col", None)),
        check_vma=False,
    )
```

profile of v0, /device:TPU:0, one launch (start us, length us, event | category | flops | bytes accessed | tf_op | source)
XLA Modules:
  0.0 134.5 jit_solution(16808524770713753963)
XLA Ops:
  7.2 0.7 all-gather.4.cloned.1.call-update
  7.9 0.8 copy.24
  8.8 3.0 %copy.32 = bf16[16,8,32,256]{3,1,2,0:T(8,128)(2,1)S(1)} copy(bf16[16,8,32,256]{3,2,1,0:T(8,128)(2,1)} %bitcast.132) | data formatting | bytes 4194304
  11.9 0.5 convolution_convert_fusion.1
  12.7 10.7 %all_gather.21 = f32[64,256]{1,0:T(8,128)S(1)} all-gather(f32[8,256]{1,0:T(8,128)S(1)} %copy-done), channel_id=1, replica_groups=mesh['row'=4,'col'=8] {'col'}, dimensions={0}, use_global_device_ids=true | all-gather | bytes 73728 | tf_op jit(solution)/shard_map/all_gather | solution.py:74
  23.6 12.4 %all-gather.4.cloned.1.call-done = bf16[64,32,256]{2,1,0:T(8,128)(2,1)} async-done(((bf16[8,32,256]{2,1,0:T(8,128)(2,1)}), bf16[64,32,256]{2,1,0:T(8,128)(2,1)}) %all-gather.4.cloned.1.call-update) | async-done | bytes 1048592 | tf_op jit(solution)/shard_map/all_gather | solution.py:73
  36.0 1.9 %copy.33 = bf16[8,8,32,256]{3,1,2,0:T(8,128)(2,1)S(1)} copy(bf16[8,8,32,256]{3,2,1,0:T(8,128)(2,1)} %bitcast.133) | data formatting | bytes 2097152
  37.9 0.5 convolution_convert_fusion
  38.7 14.9 %while.46 = (s32[]{:T(128)}, f32[8,8,256]{2,1,0:T(8,128)S(1)}, f32[8,8,256]{2,1,0:T(8,128)S(1)}, f32[8,8,256]{2,1,0:T(8,128)S(1)}, bf16[8,8,32,256]{3,2,1,0:T(8,...) while((s32[]{:T(128)}, f32[8,8,256]{2,1,0:T(8,128)S(1)}, f32[8,8,256]{2,1,0:T(8,128)S(1)}, ...), condition=%wide.region_5.6_spmd, body=%wide.region_0.5_spmd.sunk | while | flops 38658048 | bytes 4834397 | solution.py:112
  38.8 1.4 %fusion.34 = (f32[8,256]{1,0:T(8,128)S(1)}, f32[8,256,256]{1,2,0:T(8,128)S(1)}) fusion(bf16[8,8,32,256]{3,2,1,0:T(8,128)(2,1)S(1)} %get-tuple-element.407, s32[]{:T(128)} %get-tuple-element.395, bf16[8,8,32,256]{3,2,1,0:T(8,128)(2,1)S(1)} %get-tuple-element.406, f32[8,256]{1,0:T(8,128)S(1)} %get-tuple-element.362, ...), kind=kOutput, calls=%fused_computation.64.clone.1 | convolution fusion | flops 37222400 | bytes 2393088 | tf_op jit(solution)/shard_map/while/body/eval_jaxpr/gdi,gdj->gij/dot_general | solution.py:92
  40.6 1.4 %fusion.34 = (f32[8,256]{1,0:T(8,128)S(1)}, f32[8,256,256]{1,2,0:T(8,128)S(1)}) fusion(bf16[8,8,32,256]{3,2,1,0:T(8,128)(2,1)S(1)} %get-tuple-element.407, s32[]{:T(128)} %get-tuple-element.395, bf16[8,8,32,256]{3,2,1,0:T(8,128)(2,1)S(1)} %get-tuple-element.406, f32[8,256]{1,0:T(8,128)S(1)} %get-tuple-element.362, ...), kind=kOutput, calls=%fused_computation.64.clone.1 | convolution fusion | flops 37222400 | bytes 2393088 | tf_op jit(solution)/shard_map/while/body/eval_jaxpr/gdi,gdj->gij/dot_general | solution.py:92
  42.5 1.4 %fusion.34 = (f32[8,256]{1,0:T(8,128)S(1)}, f32[8,256,256]{1,2,0:T(8,128)S(1)}) fusion(bf16[8,8,32,256]{3,2,1,0:T(8,128)(2,1)S(1)} %get-tuple-element.407, s32[]{:T(128)} %get-tuple-element.395, bf16[8,8,32,256]{3,2,1,0:T(8,128)(2,1)S(1)} %get-tuple-element.406, f32[8,256]{1,0:T(8,128)S(1)} %get-tuple-element.362, ...), kind=kOutput, calls=%fused_computation.64.clone.1 | convolution fusion | flops 37222400 | bytes 2393088 | tf_op jit(solution)/shard_map/while/body/eval_jaxpr/gdi,gdj->gij/dot_general | solution.py:92
  43.9 0.3 exponential_reduce_fusion.4
  44.4 1.4 %fusion.34 = (f32[8,256]{1,0:T(8,128)S(1)}, f32[8,256,256]{1,2,0:T(8,128)S(1)}) fusion(bf16[8,8,32,256]{3,2,1,0:T(8,128)(2,1)S(1)} %get-tuple-element.407, s32[]{:T(128)} %get-tuple-element.395, bf16[8,8,32,256]{3,2,1,0:T(8,128)(2,1)S(1)} %get-tuple-element.406, f32[8,256]{1,0:T(8,128)S(1)} %get-tuple-element.362, ...), kind=kOutput, calls=%fused_computation.64.clone.1 | convolution fusion | flops 37222400 | bytes 2393088 | tf_op jit(solution)/shard_map/while/body/eval_jaxpr/gdi,gdj->gij/dot_general | solution.py:92
  46.2 1.4 %fusion.34 = (f32[8,256]{1,0:T(8,128)S(1)}, f32[8,256,256]{1,2,0:T(8,128)S(1)}) fusion(bf16[8,8,32,256]{3,2,1,0:T(8,128)(2,1)S(1)} %get-tuple-element.407, s32[]{:T(128)} %get-tuple-element.395, bf16[8,8,32,256]{3,2,1,0:T(8,128)(2,1)S(1)} %get-tuple-element.406, f32[8,256]{1,0:T(8,128)S(1)} %get-tuple-element.362, ...), kind=kOutput, calls=%fused_computation.64.clone.1 | convolution fusion | flops 37222400 | bytes 2393088 | tf_op jit(solution)/shard_map/while/body/eval_jaxpr/gdi,gdj->gij/dot_general | solution.py:92
  48.1 1.4 %fusion.34 = (f32[8,256]{1,0:T(8,128)S(1)}, f32[8,256,256]{1,2,0:T(8,128)S(1)}) fusion(bf16[8,8,32,256]{3,2,1,0:T(8,128)(2,1)S(1)} %get-tuple-element.407, s32[]{:T(128)} %get-tuple-element.395, bf16[8,8,32,256]{3,2,1,0:T(8,128)(2,1)S(1)} %get-tuple-element.406, f32[8,256]{1,0:T(8,128)S(1)} %get-tuple-element.362, ...), kind=kOutput, calls=%fused_computation.64.clone.1 | convolution fusion | flops 37222400 | bytes 2393088 | tf_op jit(solution)/shard_map/while/body/eval_jaxpr/gdi,gdj->gij/dot_general | solution.py:92
  49.5 0.3 exponential_reduce_fusion.4
  50.0 1.4 %fusion.34 = (f32[8,256]{1,0:T(8,128)S(1)}, f32[8,256,256]{1,2,0:T(8,128)S(1)}) fusion(bf16[8,8,32,256]{3,2,1,0:T(8,128)(2,1)S(1)} %get-tuple-element.407, s32[]{:T(128)} %get-tuple-element.395, bf16[8,8,32,256]{3,2,1,0:T(8,128)(2,1)S(1)} %get-tuple-element.406, f32[8,256]{1,0:T(8,128)S(1)} %get-tuple-element.362, ...), kind=kOutput, calls=%fused_computation.64.clone.1 | convolution fusion | flops 37222400 | bytes 2393088 | tf_op jit(solution)/shard_map/while/body/eval_jaxpr/gdi,gdj->gij/dot_general | solution.py:92
  51.8 1.4 %fusion.34 = (f32[8,256]{1,0:T(8,128)S(1)}, f32[8,256,256]{1,2,0:T(8,128)S(1)}) fusion(bf16[8,8,32,256]{3,2,1,0:T(8,128)(2,1)S(1)} %get-tuple-element.407, s32[]{:T(128)} %get-tuple-element.395, bf16[8,8,32,256]{3,2,1,0:T(8,128)(2,1)S(1)} %get-tuple-element.406, f32[8,256]{1,0:T(8,128)S(1)} %get-tuple-element.362, ...), kind=kOutput, calls=%fused_computation.64.clone.1 | convolution fusion | flops 37222400 | bytes 2393088 | tf_op jit(solution)/shard_map/while/body/eval_jaxpr/gdi,gdj->gij/dot_general | solution.py:92
  53.8 0.7 multiply_subtract_fusion
  54.5 9.2 %all_gather.23 = f32[128,256]{1,0:T(8,128)S(1)} all-gather(f32[16,256]{1,0:T(8,128)S(1)} %multiply_subtract_fusion), channel_id=1, replica_groups=mesh['row'=4,'col'=8] {'col'}, dimensions={0}, use_global_device_ids=true | all-gather | bytes 147456 | tf_op jit(solution)/shard_map/all_gather | solution.py:126
  63.9 14.9 %while.47 = (s32[]{:T(128)}, f32[8,8,256]{2,1,0:T(8,128)S(1)}, f32[8,8,256]{2,1,0:T(8,128)S(1)}, f32[8,8,256]{2,1,0:T(8,128)S(1)}, bf16[8,8,32,256]{3,2,1,0:T(8,...) while((s32[]{:T(128)}, f32[8,8,256]{2,1,0:T(8,128)S(1)}, f32[8,8,256]{2,1,0:T(8,128)S(1)}, ...), condition=%wide.region_13.14_spmd, body=%wide.region_8.13_spmd.sunk | while | flops 38658048 | bytes 4834397 | solution.py:140
  64.0 1.4 %fusion.35 = (f32[8,256]{1,0:T(8,128)S(1)}, f32[8,256,256]{2,1,0:T(8,128)S(1)}) fusion(bf16[8,8,32,256]{3,2,1,0:T(8,128)(2,1)S(1)} %get-tuple-element.428, s32[]{:T(128)} %get-tuple-element.416, bf16[8,8,32,256]{3,2,1,0:T(8,128)(2,1)S(1)} %get-tuple-element.427, f32[8,256]{1,0:T(8,128)S(1)} %get-tuple-element.372, ...), kind=kOutput, calls=%fused_computation.65.clone.1 | convolution fusion | flops 37222400 | bytes 2393088 | tf_op jit(solution)/shard_map/while/body/eval_jaxpr/gdi,gdj->gij/dot_general | solution.py:92
  65.5 0.3 exponential_reduce_fusion.5
  65.9 1.4 %fusion.35 = (f32[8,256]{1,0:T(8,128)S(1)}, f32[8,256,256]{2,1,0:T(8,128)S(1)}) fusion(bf16[8,8,32,256]{3,2,1,0:T(8,128)(2,1)S(1)} %get-tuple-element.428, s32[]{:T(128)} %get-tuple-element.416, bf16[8,8,32,256]{3,2,1,0:T(8,128)(2,1)S(1)} %get-tuple-element.427, f32[8,256]{1,0:T(8,128)S(1)} %get-tuple-element.372, ...), kind=kOutput, calls=%fused_computation.65.clone.1 | convolution fusion | flops 37222400 | bytes 2393088 | tf_op jit(solution)/shard_map/while/body/eval_jaxpr/gdi,gdj->gij/dot_general | solution.py:92
  67.8 1.4 %fusion.35 = (f32[8,256]{1,0:T(8,128)S(1)}, f32[8,256,256]{2,1,0:T(8,128)S(1)}) fusion(bf16[8,8,32,256]{3,2,1,0:T(8,128)(2,1)S(1)} %get-tuple-element.428, s32[]{:T(128)} %get-tuple-element.416, bf16[8,8,32,256]{3,2,1,0:T(8,128)(2,1)S(1)} %get-tuple-element.427, f32[8,256]{1,0:T(8,128)S(1)} %get-tuple-element.372, ...), kind=kOutput, calls=%fused_computation.65.clone.1 | convolution fusion | flops 37222400 | bytes 2393088 | tf_op jit(solution)/shard_map/while/body/eval_jaxpr/gdi,gdj->gij/dot_general | solution.py:92
  69.7 1.4 %fusion.35 = (f32[8,256]{1,0:T(8,128)S(1)}, f32[8,256,256]{2,1,0:T(8,128)S(1)}) fusion(bf16[8,8,32,256]{3,2,1,0:T(8,128)(2,1)S(1)} %get-tuple-element.428, s32[]{:T(128)} %get-tuple-element.416, bf16[8,8,32,256]{3,2,1,0:T(8,128)(2,1)S(1)} %get-tuple-element.427, f32[8,256]{1,0:T(8,128)S(1)} %get-tuple-element.372, ...), kind=kOutput, calls=%fused_computation.65.clone.1 | convolution fusion | flops 37222400 | bytes 2393088 | tf_op jit(solution)/shard_map/while/body/eval_jaxpr/gdi,gdj->gij/dot_general | solution.py:92
  71.5 1.4 %fusion.35 = (f32[8,256]{1,0:T(8,128)S(1)}, f32[8,256,256]{2,1,0:T(8,128)S(1)}) fusion(bf16[8,8,32,256]{3,2,1,0:T(8,128)(2,1)S(1)} %get-tuple-element.428, s32[]{:T(128)} %get-tuple-element.416, bf16[8,8,32,256]{3,2,1,0:T(8,128)(2,1)S(1)} %get-tuple-element.427, f32[8,256]{1,0:T(8,128)S(1)} %get-tuple-element.372, ...), kind=kOutput, calls=%fused_computation.65.clone.1 | convolution fusion | flops 37222400 | bytes 2393088 | tf_op jit(solution)/shard_map/while/body/eval_jaxpr/gdi,gdj->gij/dot_general | solution.py:92
  73.4 1.4 %fusion.35 = (f32[8,256]{1,0:T(8,128)S(1)}, f32[8,256,256]{2,1,0:T(8,128)S(1)}) fusion(bf16[8,8,32,256]{3,2,1,0:T(8,128)(2,1)S(1)} %get-tuple-element.428, s32[]{:T(128)} %get-tuple-element.416, bf16[8,8,32,256]{3,2,1,0:T(8,128)(2,1)S(1)} %get-tuple-element.427, f32[8,256]{1,0:T(8,128)S(1)} %get-tuple-element.372, ...), kind=kOutput, calls=%fused_computation.65.clone.1 | convolution fusion | flops 37222400 | bytes 2393088 | tf_op jit(solution)/shard_map/while/body/eval_jaxpr/gdi,gdj->gij/dot_general | solution.py:92
  75.3 1.4 %fusion.35 = (f32[8,256]{1,0:T(8,128)S(1)}, f32[8,256,256]{2,1,0:T(8,128)S(1)}) fusion(bf16[8,8,32,256]{3,2,1,0:T(8,128)(2,1)S(1)} %get-tuple-element.428, s32[]{:T(128)} %get-tuple-element.416, bf16[8,8,32,256]{3,2,1,0:T(8,128)(2,1)S(1)} %get-tuple-element.427, f32[8,256]{1,0:T(8,128)S(1)} %get-tuple-element.372, ...), kind=kOutput, calls=%fused_computation.65.clone.1 | convolution fusion | flops 37222400 | bytes 2393088 | tf_op jit(solution)/shard_map/while/body/eval_jaxpr/gdi,gdj->gij/dot_general | solution.py:92
  77.1 1.4 %fusion.35 = (f32[8,256]{1,0:T(8,128)S(1)}, f32[8,256,256]{2,1,0:T(8,128)S(1)}) fusion(bf16[8,8,32,256]{3,2,1,0:T(8,128)(2,1)S(1)} %get-tuple-element.428, s32[]{:T(128)} %get-tuple-element.416, bf16[8,8,32,256]{3,2,1,0:T(8,128)(2,1)S(1)} %get-tuple-element.427, f32[8,256]{1,0:T(8,128)S(1)} %get-tuple-element.372, ...), kind=kOutput, calls=%fused_computation.65.clone.1 | convolution fusion | flops 37222400 | bytes 2393088 | tf_op jit(solution)/shard_map/while/body/eval_jaxpr/gdi,gdj->gij/dot_general | solution.py:92
  78.9 3.7 %while.48 = (s32[]{:T(128)}, f32[2,32,256]{2,1,0:T(8,128)S(1)}, s32[64]{0:T(128)S(1)}, s32[2]{0:T(128)S(1)}, f32[8,8,256]{2,1,0:T(8,128)S(1)}, /*index=5*/s32[]{:T(128)}) while((s32[]{:T(128)}, f32[2,32,256]{2,1,0:T(8,128)S(1)}, s32[64]{0:T(128)S(1)}, s32[2]{0:T(128)S(1)}, f32[8,8,256]{2,1,0:T(8,128)S(1)}, /*index=5*/s32[]{:T(128)}) %tuple.90), condition=%wide.region_16.17_spmd, body=%wide.region_14.16_spmd.sunk | while | flops 1042466 | bytes 168537 | solution.py:55
  78.9 0.6 dynamic_slice.95
  79.5 0.6 iota_add_fusion.2
  80.2 0.5 select_reduce_fusion.2
  80.8 0.6 dynamic_slice.95
  81.3 0.6 iota_add_fusion.2
  82.1 0.5 select_reduce_fusion.2
  82.6 0.7 broadcast_in_dim_reshape.4
  83.3 3.4 %all-to-all-start = ((f32[64,1,256]{2,1,0:T(1,128)}), f32[64,1,256]{2,1,0:T(1,128)S(1)}, u32[]{:S(2)}, u32[]{:S(2)}) async-start(f32[64,1,256]{2,1,0:T(1,128)} %broadcast_in_dim_reshape.4), calls=%async_computation | async-start | bytes 131072 | tf_op jit(solution)/shard_map/all_to_all | solution.py:146
  87.1 0.7 copy.29
  87.8 3.8 %all-to-all-done = f32[64,1,256]{2,1,0:T(1,128)S(1)} async-done(((f32[64,1,256]{2,1,0:T(1,128)}), f32[64,1,256]{2,1,0:T(1,128)S(1)}, u32[]{:S(2)}, u32[]{:S(2)}) %all-to-all-start) | async-done | bytes 65568 | tf_op jit(solution)/shard_map/all_to_all | solution.py:146
  91.6 3.3 %all-to-all-start.1 = ((f32[64,1,256]{2,1,0:T(1,128)}), f32[64,1,256]{2,1,0:T(1,128)S(1)}, u32[]{:S(2)}, u32[]{:S(2)}) async-start(f32[64,1,256]{2,1,0:T(1,128)} %copy.29), calls=%async_computation.1 | async-start | bytes 131072 | tf_op jit(solution)/shard_map/all_to_all | solution.py:147
  95.0 4.9 %all-to-all-done.1 = f32[64,1,256]{2,1,0:T(1,128)S(1)} async-done(((f32[64,1,256]{2,1,0:T(1,128)}), f32[64,1,256]{2,1,0:T(1,128)S(1)}, u32[]{:S(2)}, u32[]{:S(2)}) %all-to-all-start.1) | async-done | bytes 65568 | tf_op jit(solution)/shard_map/all_to_all | solution.py:147
  100.0 13.2 %all-gather.1 = f32[32,256]{1,0:T(8,128)S(1)} all-gather(f32[8,256]{1,0:T(8,128)S(1)} %fusion.16), channel_id=3, replica_groups=mesh['row'=4,'col'=8] {'row'}, dimensions={0}, use_global_device_ids=true | all-gather | bytes 40960 | tf_op jit(solution)/shard_map/all_gather | solution.py:16
  113.1 13.1 %all-gather = f32[32,256]{1,0:T(8,128)S(1)} all-gather(f32[8,256]{1,0:T(8,128)S(1)} %reduce_max.50), channel_id=2, replica_groups=mesh['row'=4,'col'=8] {'row'}, dimensions={0}, use_global_device_ids=true | all-gather | bytes 40960 | tf_op jit(solution)/shard_map/all_gather | solution.py:16
  126.4 0.6 multiply_subtract_fusion.1
  127.0 0.7 copy.77
  (115 shorter events, 7.8 us)
Async XLA Ops:
  7.2 28.9 %all-gather.4.cloned.1.call-start = ((), (), s32[]{:S(2)}) async-start(), calls=%async_computation.2 | async-start | bytes 1179648 | tf_op jit(solution)/shard_map/all_gather | solution.py:73
  11.8 0.9 copy-start
  78.9 47.5 %copy-start.1 = (f32[8,256]{1,0:T(8,128)S(1)}, f32[8,256]{1,0:T(8,128)}, u32[]{:S(2)}) copy-start(f32[8,256]{1,0:T(8,128)} %param.17) | copy-start | bytes 24580
  83.3 8.3 %all-to-all-start = ((f32[64,1,256]{2,1,0:T(1,128)}), f32[64,1,256]{2,1,0:T(1,128)S(1)}, u32[]{:S(2)}, u32[]{:S(2)}) async-start(f32[64,1,256]{2,1,0:T(1,128)} %broadcast_in_dim_reshape.4), calls=%async_computation | async-start | bytes 131072 | tf_op jit(solution)/shard_map/all_to_all | solution.py:146
  91.6 8.3 %all-to-all-start.1 = ((f32[64,1,256]{2,1,0:T(1,128)}), f32[64,1,256]{2,1,0:T(1,128)S(1)}, u32[]{:S(2)}, u32[]{:S(2)}) async-start(f32[64,1,256]{2,1,0:T(1,128)} %copy.29), calls=%async_computation.1 | async-start | bytes 131072 | tf_op jit(solution)/shard_map/all_to_all | solution.py:147
Sparse Core Ops, SparseCore 0:
  9.9 26.1 all-gather.3
where the time goes:
time: 135 us
  blocking collectives  46.2 us (34%)
  matrix products  24.2 us (18%)
  waiting for transfers between devices  21.8 us (16%)
  between operations  14.3 us (11%)
  other arithmetic  10.1 us (7%)
  local copies, waits for them, and re-layouts  10.1 us (7%)
  starting transfers between devices  6.74 us (5%)
    all_gather x2, blocking collectives, joined(): pieces = jax.tree.map(lambda part: lax.all_gather(part, axis), value)  26.3 us
    dot_general x16, matrix products, distances(): jnp.einsum('gdi,gdj->gij', src_block, tgt_block, preferred_element_type=j...  22.4 us
    all_gather x1, waiting for transfers between devices, on_device(): all_points = lax.all_gather(tgt_points, 'col', axis=0, tiled=True)  12.4 us
    all_gather x1, blocking collectives, on_device(): all_potential = lax.all_gather(tgt_potential, 'col', axis=0, tiled=True)  10.7 us
    all_gather x1, blocking collectives, on_device(): src_new = lax.all_gather(own_new, 'col', axis=0, tiled=True)  9.15 us
    unnamed x8, local copies, waits for them, and re-layouts  6.32 us
    all_to_all x1, waiting for transfers between devices, on_device(): lax.all_to_all(target_total[:, None, :], 'col', split_axis=0, concat_axis...  4.89 us
    all_to_all x1, waiting for transfers between devices, on_device(): lax.all_to_all(target_top[:, None, :], 'col', split_axis=0, concat_axis=1...  3.85 us
  transfers between devices with their start and end apart: 3, of which 3 were waited for; matrix products, arithmetic and copies ran while one was open for 5% of the time, Pallas kernels for 0%

commit v1 on v0

--- a/solution.py
+++ b/solution.py
@@ -1,8 +1,10 @@
+import functools
 import math
 import jax
 import jax.numpy as jnp
 from jax import lax
 from jax.sharding import PartitionSpec as P
+from jax.lax import all_to_all, axis_size
 
 DIM = 32
 FANOUT = 4
@@ -10,6 +12,17 @@
 epsilon = 0.1
 very_low = -1e30
 entry_batch = 8
+
+
+def lay_the_vector(local_array, ax_name, axis_no, pos_dim):
+    carry = axis_size(ax_name)
+    w2 = jnp.split(local_array, carry, axis_no)
+    z_new = jnp.stack(w2, axis=0)
+    u_next = all_to_all(z_new, ax_name, 0, 0)
+    return jnp.concatenate(u_next, pos_dim)
+
+
+_order_teams = functools.partial(lay_the_vector, ax_name="col", axis_no=0, pos_dim=1)
 
 
 def joined(value, axis, join):
@@ -144,7 +157,7 @@
     target_top, target_total = collect_rows(tgt_rows, slot_tgt, column_top, column_total)
     sent_top, sent_total = (
         lax.all_to_all(target_top[:, None, :], "col", split_axis=0, concat_axis=1, tiled=True),
-        lax.all_to_all(target_total[:, None, :], "col", split_axis=0, concat_axis=1, tiled=True),
+        _order_teams(target_total[:, None, :]),
     )
     local_top = jnp.max(sent_top, axis=1)
     local_total = jnp.sum(sent_total * jnp.exp(sent_top - local_top[:, None, :]), axis=1)

time: 135 us -> 140 us (1.037)
  local copies, waits for them, and re-layouts: 10.1 us -> 14.1 us
    unnamed x8 -> x15, local copies, waits for them, and re-layouts: 6.32 us -> 10.5 us
  transfers between devices with their start and end apart: 3 -> 3, of which waited for: 3 -> 3; matrix products, arithmetic and copies ran while one was open for 5% -> 4% of each run, Pallas kernels for 0% -> 0%
where the time goes in v1:
time: 140 us; the launch traced here: 139 us
  blocking collectives  46.2 us (33%)
  matrix products  24.2 us (17%)
  waiting for transfers between devices  22.3 us (16%)
  between operations  14.3 us (10%)
  local copies, waits for them, and re-layouts  14.1 us (10%)
  other arithmetic  10.1 us (7%)
  starting transfers between devices  6.74 us (5%)
    all_gather x2, blocking collectives, joined(): pieces = jax.tree.map(lambda part: lax.all_gather(part, axis), value)  26.3 us
    dot_general x16, matrix products, distances(): jnp.einsum('gdi,gdj->gij', src_block, tgt_block, preferred_element_type=j...  22.4 us
    all_gather x1, waiting for transfers between devices, on_device(): all_points = lax.all_gather(tgt_points, 'col', axis=0, tiled=True)  12.4 us
    all_gather x1, blocking collectives, on_device(): all_potential = lax.all_gather(tgt_potential, 'col', axis=0, tiled=True)  10.7 us
    unnamed x15, local copies, waits for them, and re-layouts  10.5 us
    all_gather x1, blocking collectives, on_device(): src_new = lax.all_gather(own_new, 'col', axis=0, tiled=True)  9.15 us
    all_to_all x1, waiting for transfers between devices, lay_the_vector(): u_next = all_to_all(z_new, ax_name, 0, 0)  4.93 us
    all_to_all x1, waiting for transfers between devices, on_device(): lax.all_to_all(target_top[:, None, :], 'col', split_axis=0, concat_axis=1...  4.35 us
  transfers between devices with their start and end apart: 3, of which 3 were waited for; matrix products, arithmetic and copies ran while one was open for 4% of the time, Pallas kernels for 0%

profile of v1, /device:TPU:0, one launch (start us, length us, event | category | flops | bytes accessed | tf_op | source)
XLA Modules:
  0.0 139.1 jit_solution(10275742157607524991)
XLA Ops:
  7.2 0.7 all-gather.4.cloned.1.call-update
  7.9 0.8 copy.22
  8.8 3.0 %copy.28 = bf16[16,8,32,256]{3,1,2,0:T(8,128)(2,1)S(1)} copy(bf16[16,8,32,256]{3,2,1,0:T(8,128)(2,1)} %bitcast.164) | data formatting | bytes 4194304
  12.7 10.7 %all_gather.21 = f32[64,256]{1,0:T(8,128)S(1)} all-gather(f32[8,256]{1,0:T(8,128)S(1)} %copy-done), channel_id=1, replica_groups=mesh['row'=4,'col'=8] {'col'}, dimensions={0}, use_global_device_ids=true | all-gather | bytes 73728 | tf_op jit(solution)/shard_map/all_gather | solution.py:87
  23.6 12.4 %all-gather.4.cloned.1.call-done = bf16[64,32,256]{2,1,0:T(8,128)(2,1)} async-done(((bf16[8,32,256]{2,1,0:T(8,128)(2,1)}), bf16[64,32,256]{2,1,0:T(8,128)(2,1)}) %all-gather.4.cloned.1.call-update) | async-done | bytes 1048592 | tf_op jit(solution)/shard_map/all_gather | solution.py:86
  36.0 1.9 %copy.29 = bf16[8,8,32,256]{3,1,2,0:T(8,128)(2,1)S(1)} copy(bf16[8,8,32,256]{3,2,1,0:T(8,128)(2,1)} %bitcast.165) | data formatting | bytes 2097152
  38.7 14.9 %while.46 = (s32[]{:T(128)}, f32[8,8,256]{2,1,0:T(8,128)S(1)}, f32[8,8,256]{2,1,0:T(8,128)S(1)}, f32[8,8,256]{2,1,0:T(8,128)S(1)}, bf16[8,8,32,256]{3,2,1,0:T(8,...) while((s32[]{:T(128)}, f32[8,8,256]{2,1,0:T(8,128)S(1)}, f32[8,8,256]{2,1,0:T(8,128)S(1)}, ...), condition=%wide.region_5.6_spmd, body=%wide.region_0.5_spmd.sunk | while | flops 38658048 | bytes 4834397 | solution.py:125
  38.8 1.4 %fusion.35 = (f32[8,256]{1,0:T(8,128)S(1)}, f32[8,256,256]{1,2,0:T(8,128)S(1)}) fusion(bf16[8,8,32,256]{3,2,1,0:T(8,128)(2,1)S(1)} %get-tuple-element.407, s32[]{:T(128)} %get-tuple-element.395, bf16[8,8,32,256]{3,2,1,0:T(8,128)(2,1)S(1)} %get-tuple-element.406, f32[8,256]{1,0:T(8,128)S(1)} %get-tuple-element.362, ...), kind=kOutput, calls=%fused_computation.81.clone.1 | convolution fusion | flops 37222400 | bytes 2393088 | tf_op jit(solution)/shard_map/while/body/eval_jaxpr/gdi,gdj->gij/dot_general | solution.py:105
  40.6 1.4 %fusion.35 = (f32[8,256]{1,0:T(8,128)S(1)}, f32[8,256,256]{1,2,0:T(8,128)S(1)}) fusion(bf16[8,8,32,256]{3,2,1,0:T(8,128)(2,1)S(1)} %get-tuple-element.407, s32[]{:T(128)} %get-tuple-element.395, bf16[8,8,32,256]{3,2,1,0:T(8,128)(2,1)S(1)} %get-tuple-element.406, f32[8,256]{1,0:T(8,128)S(1)} %get-tuple-element.362, ...), kind=kOutput, calls=%fused_computation.81.clone.1 | convolution fusion | flops 37222400 | bytes 2393088 | tf_op jit(solution)/shard_map/while/body/eval_jaxpr/gdi,gdj->gij/dot_general | solution.py:105
  42.5 1.4 %fusion.35 = (f32[8,256]{1,0:T(8,128)S(1)}, f32[8,256,256]{1,2,0:T(8,128)S(1)}) fusion(bf16[8,8,32,256]{3,2,1,0:T(8,128)(2,1)S(1)} %get-tuple-element.407, s32[]{:T(128)} %get-tuple-element.395, bf16[8,8,32,256]{3,2,1,0:T(8,128)(2,1)S(1)} %get-tuple-element.406, f32[8,256]{1,0:T(8,128)S(1)} %get-tuple-element.362, ...), kind=kOutput, calls=%fused_computation.81.clone.1 | convolution fusion | flops 37222400 | bytes 2393088 | tf_op jit(solution)/shard_map/while/body/eval_jaxpr/gdi,gdj->gij/dot_general | solution.py:105
  44.4 1.4 %fusion.35 = (f32[8,256]{1,0:T(8,128)S(1)}, f32[8,256,256]{1,2,0:T(8,128)S(1)}) fusion(bf16[8,8,32,256]{3,2,1,0:T(8,128)(2,1)S(1)} %get-tuple-element.407, s32[]{:T(128)} %get-tuple-element.395, bf16[8,8,32,256]{3,2,1,0:T(8,128)(2,1)S(1)} %get-tuple-element.406, f32[8,256]{1,0:T(8,128)S(1)} %get-tuple-element.362, ...), kind=kOutput, calls=%fused_computation.81.clone.1 | convolution fusion | flops 37222400 | bytes 2393088 | tf_op jit(solution)/shard_map/while/body/eval_jaxpr/gdi,gdj->gij/dot_general | solution.py:105
  46.2 1.4 %fusion.35 = (f32[8,256]{1,0:T(8,128)S(1)}, f32[8,256,256]{1,2,0:T(8,128)S(1)}) fusion(bf16[8,8,32,256]{3,2,1,0:T(8,128)(2,1)S(1)} %get-tuple-element.407, s32[]{:T(128)} %get-tuple-element.395, bf16[8,8,32,256]{3,2,1,0:T(8,128)(2,1)S(1)} %get-tuple-element.406, f32[8,256]{1,0:T(8,128)S(1)} %get-tuple-element.362, ...), kind=kOutput, calls=%fused_computation.81.clone.1 | convolution fusion | flops 37222400 | bytes 2393088 | tf_op jit(solution)/shard_map/while/body/eval_jaxpr/gdi,gdj->gij/dot_general | solution.py:105
  48.1 1.4 %fusion.35 = (f32[8,256]{1,0:T(8,128)S(1)}, f32[8,256,256]{1,2,0:T(8,128)S(1)}) fusion(bf16[8,8,32,256]{3,2,1,0:T(8,128)(2,1)S(1)} %get-tuple-element.407, s32[]{:T(128)} %get-tuple-element.395, bf16[8,8,32,256]{3,2,1,0:T(8,128)(2,1)S(1)} %get-tuple-element.406, f32[8,256]{1,0:T(8,128)S(1)} %get-tuple-element.362, ...), kind=kOutput, calls=%fused_computation.81.clone.1 | convolution fusion | flops 37222400 | bytes 2393088 | tf_op jit(solution)/shard_map/while/body/eval_jaxpr/gdi,gdj->gij/dot_general | solution.py:105
  50.0 1.4 %fusion.35 = (f32[8,256]{1,0:T(8,128)S(1)}, f32[8,256,256]{1,2,0:T(8,128)S(1)}) fusion(bf16[8,8,32,256]{3,2,1,0:T(8,128)(2,1)S(1)} %get-tuple-element.407, s32[]{:T(128)} %get-tuple-element.395, bf16[8,8,32,256]{3,2,1,0:T(8,128)(2,1)S(1)} %get-tuple-element.406, f32[8,256]{1,0:T(8,128)S(1)} %get-tuple-element.362, ...), kind=kOutput, calls=%fused_computation.81.clone.1 | convolution fusion | flops 37222400 | bytes 2393088 | tf_op jit(solution)/shard_map/while/body/eval_jaxpr/gdi,gdj->gij/dot_general | solution.py:105
  51.8 1.4 %fusion.35 = (f32[8,256]{1,0:T(8,128)S(1)}, f32[8,256,256]{1,2,0:T(8,128)S(1)}) fusion(bf16[8,8,32,256]{3,2,1,0:T(8,128)(2,1)S(1)} %get-tuple-element.407, s32[]{:T(128)} %get-tuple-element.395, bf16[8,8,32,256]{3,2,1,0:T(8,128)(2,1)S(1)} %get-tuple-element.406, f32[8,256]{1,0:T(8,128)S(1)} %get-tuple-element.362, ...), kind=kOutput, calls=%fused_computation.81.clone.1 | convolution fusion | flops 37222400 | bytes 2393088 | tf_op jit(solution)/shard_map/while/body/eval_jaxpr/gdi,gdj->gij/dot_general | solution.py:105
  53.8 0.7 multiply_subtract_fusion
  54.5 9.2 %all_gather.23 = f32[128,256]{1,0:T(8,128)S(1)} all-gather(f32[16,256]{1,0:T(8,128)S(1)} %multiply_subtract_fusion), channel_id=1, replica_groups=mesh['row'=4,'col'=8] {'col'}, dimensions={0}, use_global_device_ids=true | all-gather | bytes 147456 | tf_op jit(solution)/shard_map/all_gather | solution.py:139
  63.9 14.9 %while.47 = (s32[]{:T(128)}, f32[8,8,256]{2,1,0:T(8,128)S(1)}, f32[8,8,256]{2,1,0:T(8,128)S(1)}, f32[8,8,256]{2,1,0:T(8,128)S(1)}, bf16[8,8,32,256]{3,2,1,0:T(8,...) while((s32[]{:T(128)}, f32[8,8,256]{2,1,0:T(8,128)S(1)}, f32[8,8,256]{2,1,0:T(8,128)S(1)}, ...), condition=%wide.region_13.14_spmd, body=%wide.region_8.13_spmd.sunk | while | flops 38658048 | bytes 4834397 | solution.py:153
  64.0 1.4 %fusion.36 = (f32[8,256]{1,0:T(8,128)S(1)}, f32[8,256,256]{2,1,0:T(8,128)S(1)}) fusion(bf16[8,8,32,256]{3,2,1,0:T(8,128)(2,1)S(1)} %get-tuple-element.428, s32[]{:T(128)} %get-tuple-element.416, bf16[8,8,32,256]{3,2,1,0:T(8,128)(2,1)S(1)} %get-tuple-element.427, f32[8,256]{1,0:T(8,128)S(1)} %get-tuple-element.372, ...), kind=kOutput, calls=%fused_computation.82.clone.1 | convolution fusion | flops 37222400 | bytes 2393088 | tf_op jit(solution)/shard_map/while/body/eval_jaxpr/gdi,gdj->gij/dot_general | solution.py:105
  65.9 1.4 %fusion.36 = (f32[8,256]{1,0:T(8,128)S(1)}, f32[8,256,256]{2,1,0:T(8,128)S(1)}) fusion(bf16[8,8,32,256]{3,2,1,0:T(8,128)(2,1)S(1)} %get-tuple-element.428, s32[]{:T(128)} %get-tuple-element.416, bf16[8,8,32,256]{3,2,1,0:T(8,128)(2,1)S(1)} %get-tuple-element.427, f32[8,256]{1,0:T(8,128)S(1)} %get-tuple-element.372, ...), kind=kOutput, calls=%fused_computation.82.clone.1 | convolution fusion | flops 37222400 | bytes 2393088 | tf_op jit(solution)/shard_map/while/body/eval_jaxpr/gdi,gdj->gij/dot_general | solution.py:105
  67.8 1.4 %fusion.36 = (f32[8,256]{1,0:T(8,128)S(1)}, f32[8,256,256]{2,1,0:T(8,128)S(1)}) fusion(bf16[8,8,32,256]{3,2,1,0:T(8,128)(2,1)S(1)} %get-tuple-element.428, s32[]{:T(128)} %get-tuple-element.416, bf16[8,8,32,256]{3,2,1,0:T(8,128)(2,1)S(1)} %get-tuple-element.427, f32[8,256]{1,0:T(8,128)S(1)} %get-tuple-element.372, ...), kind=kOutput, calls=%fused_computation.82.clone.1 | convolution fusion | flops 37222400 | bytes 2393088 | tf_op jit(solution)/shard_map/while/body/eval_jaxpr/gdi,gdj->gij/dot_general | solution.py:105
  69.7 1.4 %fusion.36 = (f32[8,256]{1,0:T(8,128)S(1)}, f32[8,256,256]{2,1,0:T(8,128)S(1)}) fusion(bf16[8,8,32,256]{3,2,1,0:T(8,128)(2,1)S(1)} %get-tuple-element.428, s32[]{:T(128)} %get-tuple-element.416, bf16[8,8,32,256]{3,2,1,0:T(8,128)(2,1)S(1)} %get-tuple-element.427, f32[8,256]{1,0:T(8,128)S(1)} %get-tuple-element.372, ...), kind=kOutput, calls=%fused_computation.82.clone.1 | convolution fusion | flops 37222400 | bytes 2393088 | tf_op jit(solution)/shard_map/while/body/eval_jaxpr/gdi,gdj->gij/dot_general | solution.py:105
  71.5 1.4 %fusion.36 = (f32[8,256]{1,0:T(8,128)S(1)}, f32[8,256,256]{2,1,0:T(8,128)S(1)}) fusion(bf16[8,8,32,256]{3,2,1,0:T(8,128)(2,1)S(1)} %get-tuple-element.428, s32[]{:T(128)} %get-tuple-element.416, bf16[8,8,32,256]{3,2,1,0:T(8,128)(2,1)S(1)} %get-tuple-element.427, f32[8,256]{1,0:T(8,128)S(1)} %get-tuple-element.372, ...), kind=kOutput, calls=%fused_computation.82.clone.1 | convolution fusion | flops 37222400 | bytes 2393088 | tf_op jit(solution)/shard_map/while/body/eval_jaxpr/gdi,gdj->gij/dot_general | solution.py:105
  73.4 1.4 %fusion.36 = (f32[8,256]{1,0:T(8,128)S(1)}, f32[8,256,256]{2,1,0:T(8,128)S(1)}) fusion(bf16[8,8,32,256]{3,2,1,0:T(8,128)(2,1)S(1)} %get-tuple-element.428, s32[]{:T(128)} %get-tuple-element.416, bf16[8,8,32,256]{3,2,1,0:T(8,128)(2,1)S(1)} %get-tuple-element.427, f32[8,256]{1,0:T(8,128)S(1)} %get-tuple-element.372, ...), kind=kOutput, calls=%fused_computation.82.clone.1 | convolution fusion | flops 37222400 | bytes 2393088 | tf_op jit(solution)/shard_map/while/body/eval_jaxpr/gdi,gdj->gij/dot_general | solution.py:105
  75.3 1.4 %fusion.36 = (f32[8,256]{1,0:T(8,128)S(1)}, f32[8,256,256]{2,1,0:T(8,128)S(1)}) fusion(bf16[8,8,32,256]{3,2,1,0:T(8,128)(2,1)S(1)} %get-tuple-element.428, s32[]{:T(128)} %get-tuple-element.416, bf16[8,8,32,256]{3,2,1,0:T(8,128)(2,1)S(1)} %get-tuple-element.427, f32[8,256]{1,0:T(8,128)S(1)} %get-tuple-element.372, ...), kind=kOutput, calls=%fused_computation.82.clone.1 | convolution fusion | flops 37222400 | bytes 2393088 | tf_op jit(solution)/shard_map/while/body/eval_jaxpr/gdi,gdj->gij/dot_general | solution.py:105
  77.1 1.4 %fusion.36 = (f32[8,256]{1,0:T(8,128)S(1)}, f32[8,256,256]{2,1,0:T(8,128)S(1)}) fusion(bf16[8,8,32,256]{3,2,1,0:T(8,128)(2,1)S(1)} %get-tuple-element.428, s32[]{:T(128)} %get-tuple-element.416, bf16[8,8,32,256]{3,2,1,0:T(8,128)(2,1)S(1)} %get-tuple-element.427, f32[8,256]{1,0:T(8,128)S(1)} %get-tuple-element.372, ...), kind=kOutput, calls=%fused_computation.82.clone.1 | convolution fusion | flops 37222400 | bytes 2393088 | tf_op jit(solution)/shard_map/while/body/eval_jaxpr/gdi,gdj->gij/dot_general | solution.py:105
  78.9 3.7 %while.48 = (s32[]{:T(128)}, f32[2,32,256]{2,1,0:T(8,128)S(1)}, s32[64]{0:T(128)S(1)}, s32[2]{0:T(128)S(1)}, f32[8,8,256]{2,1,0:T(8,128)S(1)}, /*index=5*/s32[]{:T(128)}) while((s32[]{:T(128)}, f32[2,32,256]{2,1,0:T(8,128)S(1)}, s32[64]{0:T(128)S(1)}, s32[2]{0:T(128)S(1)}, f32[8,8,256]{2,1,0:T(8,128)S(1)}, /*index=5*/s32[]{:T(128)}) %tuple.90), condition=%wide.region_16.17_spmd, body=%wide.region_14.16_spmd.sunk | while | flops 1042466 | bytes 168537 | solution.py:68
  78.9 0.6 dynamic_slice.95
  79.5 0.6 iota_add_fusion.2
  80.8 0.6 dynamic_slice.95
  81.3 0.6 iota_add_fusion.2
  82.6 0.7 broadcast_in_dim_reshape.4
  83.7 0.6 constant_dynamic-update-slice_fusion.7
  84.3 0.6 constant_dynamic-update-slice_fusion.6
  84.9 0.6 constant_dynamic-update-slice_fusion.5
  85.5 0.6 constant_dynamic-update-slice_fusion.4
  86.1 0.6 constant_dynamic-update-slice_fusion.3
  86.7 0.6 constant_dynamic-update-slice_fusion.2
  87.3 0.6 constant_dynamic-update-slice_fusion.1
  87.9 3.4 %all-to-all-start = ((f32[64,1,256]{2,1,0:T(1,128)}), f32[64,1,256]{2,1,0:T(1,128)S(1)}, u32[]{:S(2)}, u32[]{:S(2)}) async-start(f32[64,1,256]{2,1,0:T(1,128)} %broadcast_in_dim_reshape.4), calls=%async_computation | async-start | bytes 131072 | tf_op jit(solution)/shard_map/all_to_all | solution.py:159
  91.2 0.6 constant_dynamic-update-slice_fusion
  91.8 4.3 %all-to-all-done = f32[64,1,256]{2,1,0:T(1,128)S(1)} async-done(((f32[64,1,256]{2,1,0:T(1,128)}), f32[64,1,256]{2,1,0:T(1,128)S(1)}, u32[]{:S(2)}, u32[]{:S(2)}) %all-to-all-start) | async-done | bytes 65568 | tf_op jit(solution)/shard_map/all_to_all | solution.py:159
  96.2 3.3 %all-to-all-start.1 = ((f32[8,8,1,256]{3,1,2,0:T(8,128)}), f32[8,8,1,256]{3,1,2,0:T(8,128)S(1)}, u32[]{:S(2)}, u32[]{:S(2)}) async-start(f32[8,8,1,256]{3,1,2,0:T(8,128)} %constant_dynamic-update-slice_fusion), calls=%async_computation.1 | async-start | bytes 131072 | tf_op jit(solution)/shard_map/all_to_all | solution.py:21
  99.6 4.9 %all-to-all-done.1 = f32[8,8,1,256]{3,1,2,0:T(8,128)S(1)} async-done(((f32[8,8,1,256]{3,1,2,0:T(8,128)}), f32[8,8,1,256]{3,1,2,0:T(8,128)S(1)}, u32[]{:S(2)}, u32[]{:S(2)}) %all-to-all-start.1) | async-done | bytes 65568 | tf_op jit(solution)/shard_map/all_to_all | solution.py:21
  104.5 13.2 %all-gather.1 = f32[32,256]{1,0:T(8,128)S(1)} all-gather(f32[8,256]{1,0:T(8,128)S(1)} %fusion.16), channel_id=3, replica_groups=mesh['row'=4,'col'=8] {'row'}, dimensions={0}, use_global_device_ids=true | all-gather | bytes 40960 | tf_op jit(solution)/shard_map/all_gather | solution.py:29
  117.7 13.1 %all-gather = f32[32,256]{1,0:T(8,128)S(1)} all-gather(f32[8,256]{1,0:T(8,128)S(1)} %bitcast_reduce_fusion), channel_id=2, replica_groups=mesh['row'=4,'col'=8] {'row'}, dimensions={0}, use_global_device_ids=true | all-gather | bytes 40960 | tf_op jit(solution)/shard_map/all_gather | solution.py:29
  131.0 0.6 multiply_subtract_fusion.1
  131.6 0.7 copy.80
  (122 shorter events, 10.6 us)
Async XLA Ops:
  7.2 28.9 %all-gather.4.cloned.1.call-start = ((), (), s32[]{:S(2)}) async-start(), calls=%async_computation.2 | async-start | bytes 1179648 | tf_op jit(solution)/shard_map/all_gather | solution.py:86
  11.8 0.9 copy-start
  78.9 52.1 %copy-start.1 = (f32[8,256]{1,0:T(8,128)S(1)}, f32[8,256]{1,0:T(8,128)}, u32[]{:S(2)}) copy-start(f32[8,256]{1,0:T(8,128)} %param.17) | copy-start | bytes 24580
  87.9 8.3 %all-to-all-start = ((f32[64,1,256]{2,1,0:T(1,128)}), f32[64,1,256]{2,1,0:T(1,128)S(1)}, u32[]{:S(2)}, u32[]{:S(2)}) async-start(f32[64,1,256]{2,1,0:T(1,128)} %broadcast_in_dim_reshape.4), calls=%async_computation | async-start | bytes 131072 | tf_op jit(solution)/shard_map/all_to_all | solution.py:159
  96.2 8.3 %all-to-all-start.1 = ((f32[8,8,1,256]{3,1,2,0:T(8,128)}), f32[8,8,1,256]{3,1,2,0:T(8,128)S(1)}, u32[]{:S(2)}, u32[]{:S(2)}) async-start(f32[8,8,1,256]{3,1,2,0:T(8,128)} %constant_dynamic-update-slice_fusion), calls=%async_computation.1 | async-start | bytes 131072 | tf_op jit(solution)/shard_map/all_to_all | solution.py:21
Sparse Core Ops, SparseCore 0:
  9.9 26.1 all-gather.3
